TPU v7x, 32 devices: a whole 2x2x4 slice. The times are simulated.
32 devices in a mesh: dp: 4 (over x, core), tensor: 8 (over z, y).
Axes of the slice: x: 2, y: 2, z: 4, core: 2. Of those that a mesh axis runs over, the one named last changes fastest.
Arguments:
- tokens: bfloat16 [8192, 1024], P('dp'), may hold values from -6 to 6
- segment_ids: int32 [4, 2048], P('dp'), may hold values from 0 to 7, never falling along the last dimension, each value on 1 to 512 neighbouring positions
- first_gain: bfloat16 [1024], replicated, may hold values from 0.5 to 1.5
- first_shift: bfloat16 [1024], replicated, may hold values from -3 to 3
- qkv_weight: bfloat16 [1024, 16, 192], P(None, 'tensor'), may hold values from -0.1875 to 0.1875
- qv_bias: bfloat16 [16, 128], P('tensor'), may hold values from -3 to 3
- out_weight: bfloat16 [1024, 1024], P('tensor'), may hold values from -0.5 to 0.5
- out_bias: bfloat16 [1024], replicated, may hold values from -2 to 2
- second_gain: bfloat16 [1024], replicated, may hold values from 0.5 to 1.5
- second_shift: bfloat16 [1024], replicated, may hold values from -3 to 3
- up_weight: bfloat16 [1024, 4096], P(None, 'tensor'), may hold values from -0.1875 to 0.1875
- up_bias: bfloat16 [4096], P('tensor'), may hold values from -3 to 3
- down_weight: bfloat16 [4096, 1024], P('tensor'), may hold values from -0.125 to 0.125
- down_bias: bfloat16 [1024], replicated, may hold values from -2 to 2
- cotangent: bfloat16 [8192, 1024], P('dp'), may hold values from -6 to 6
Outputs:
- output: bfloat16 [8192, 1024], P('dp')
- grad_tokens: bfloat16 [8192, 1024], P('dp')
- grad_first_gain: float32 [1024], replicated
- grad_first_shift: float32 [1024], replicated
- grad_qkv_weight: float32 [1024, 16, 192], P(None, 'tensor')
- grad_qv_bias: float32 [16, 128], P('tensor')
- grad_out_weight: float32 [1024, 1024], P('tensor')
- grad_out_bias: float32 [1024], replicated
- grad_second_gain: float32 [1024], replicated
- grad_second_shift: float32 [1024], replicated
- grad_up_weight: float32 [1024, 4096], P(None, 'tensor')
- grad_up_bias: float32 [4096], P('tensor')
- grad_down_weight: float32 [4096, 1024], P('tensor')
- grad_down_bias: float32 [1024], replicated
Inputs may be any that keep to these rules, and one draw needn't show every extreme that they name: `segment_ids`: each row of 2048 positions is cut into documents of consecutive positions, at most 512 long, one exactly that long; ids never fall along a row.
All inputs are finite; a program needn't handle non-finite values.
Results may differ from a plain program's by a relative error of at most 0.023.
Values may be sent and summed in bfloat16 or wider, within the bound.
A program may use at most 128 MiB of HBM per device.

v0:
```python
import math
import jax
import jax.numpy as jnp
from jax import lax
from jax.sharding import PartitionSpec as P

norm_eps = 1e-05


def layer_norm(values, gain_vec, shift_vec):
    center = jnp.mean(values, axis=-1, keepdims=True)
    offset = values - center
    spread = jnp.mean(offset * offset, axis=-1, keepdims=True)
    return offset * lax.rsqrt(spread + norm_eps) * gain_vec + shift_vec


def gelu_tanh(values):
    return (
        0.5
        * values
        * (1.0 + jnp.tanh(0.7978845608028654 * (values + 0.044715 * values * values * values)))
    )


def head_slopes(local_heads):
    total = local_heads * lax.axis_size("tensor")
    first = lax.axis_index("tensor") * local_heads
    heads_idx = first + jnp.arange(local_heads, dtype=jnp.int32)
    return jnp.exp2(-8.0 * (heads_idx + 1).astype(jnp.float32) / total)


def block_scores(query_blk, keys, start, seg_row, slopes):
    rows = query_blk.shape[0]
    length = keys.shape[0]
    scale = 1.0 / math.sqrt(keys.shape[2])
    raw = jnp.einsum("qhe,khe->hqk", query_blk, keys, preferred_element_type=jnp.float32) * scale
    query_pos = start + jnp.arange(rows, dtype=jnp.int32)
    key_pos = jnp.arange(length, dtype=jnp.int32)
    distance = (query_pos[:, None] - key_pos[None, :]).astype(jnp.float32)
    raw = raw - slopes[:, None, None] * distance[None]
    query_seg = lax.dynamic_slice_in_dim(seg_row, start, rows, 0)
    allowed = (query_seg[:, None] == seg_row[None, :]) & (key_pos[None, :] <= query_pos[:, None])
    return jnp.where(allowed[None], raw, -1e30)


def attend_forward(query, keys, values, seg_row, slopes):
    length = query.shape[0]
    block = min(512, length)

    def one_block(index):
        start = index * block
        query_blk = lax.dynamic_slice_in_dim(query, start, block, 0)
        scores = block_scores(query_blk, keys, start, seg_row, slopes)
        peak = jnp.max(scores, axis=-1, keepdims=True)
        expo = jnp.exp(scores - peak)
        total = jnp.sum(expo, axis=-1, keepdims=True)
        weights_low = (expo / total).astype(jnp.bfloat16)
        ctx_blk = jnp.einsum(
            "hqk,khe->qhe", weights_low, values, preferred_element_type=jnp.float32
        )
        return (ctx_blk, (peak + jnp.log(total))[:, :, 0])

    ctx_blocks, lse_blocks = lax.map(one_block, jnp.arange(length // block, dtype=jnp.int32))
    return (ctx_blocks.reshape(query.shape), lse_blocks)


def attend_backward(query, keys, values, seg_row, slopes, lse_blocks, grad_context):
    length = query.shape[0]
    block = min(512, length)
    scale = 1.0 / math.sqrt(keys.shape[2])

    def one_block(carry, index):
        grad_keys, grad_values = carry
        start = index * block
        query_blk = lax.dynamic_slice_in_dim(query, start, block, 0)
        grad_blk = lax.dynamic_slice_in_dim(grad_context, start, block, 0)
        scores = block_scores(query_blk, keys, start, seg_row, slopes)
        probs = jnp.exp(scores - lse_blocks[index][:, :, None])
        probs_low = probs.astype(jnp.bfloat16)
        grad_probs = jnp.einsum(
            "qhe,khe->hqk", grad_blk, values, preferred_element_type=jnp.float32
        )
        inner = jnp.sum(probs * grad_probs, axis=-1, keepdims=True)
        grad_scores = (probs * (grad_probs - inner)).astype(jnp.bfloat16)
        grad_query = (
            jnp.einsum("hqk,khe->qhe", grad_scores, keys, preferred_element_type=jnp.float32)
            * scale
        )
        grad_keys = (
            grad_keys
            + jnp.einsum("hqk,qhe->khe", grad_scores, query_blk, preferred_element_type=jnp.float32)
            * scale
        )
        grad_values = grad_values + jnp.einsum(
            "hqk,qhe->khe", probs_low, grad_blk, preferred_element_type=jnp.float32
        )
        return ((grad_keys, grad_values), grad_query)

    empty = jnp.zeros(keys.shape, jnp.float32)
    (grad_keys, grad_values), grad_query = lax.scan(
        one_block, (empty, empty), jnp.arange(length // block, dtype=jnp.int32)
    )
    return (grad_query.reshape(query.shape), grad_keys, grad_values)


def attn_front(
    tokens_f, seg_row, first_gain, first_shift, qkv_weight, qv_bias, out_weight, out_bias
):
    length = tokens_f.shape[0]
    normed_low = layer_norm(
        tokens_f, first_gain.astype(jnp.float32), first_shift.astype(jnp.float32)
    ).astype(jnp.bfloat16)
    merged = jnp.einsum("td,dhe->the", normed_low, qkv_weight, preferred_element_type=jnp.float32)
    width = merged.shape[2] // 3
    bias_f = qv_bias.astype(jnp.float32)
    query = (merged[:, :, :width] + bias_f[:, :width]).astype(jnp.bfloat16)
    keys = merged[:, :, width : 2 * width].astype(jnp.bfloat16)
    values = (merged[:, :, 2 * width :] + bias_f[:, width:]).astype(jnp.bfloat16)
    slopes = head_slopes(query.shape[1])
    context, lse_blocks = attend_forward(query, keys, values, seg_row, slopes)
    context_low = context.reshape(length, -1).astype(jnp.bfloat16)
    partial_out = jnp.dot(context_low, out_weight, preferred_element_type=jnp.float32).astype(
        jnp.bfloat16
    )
    mixed = lax.psum(partial_out, "tensor").astype(jnp.float32)
    middle = tokens_f + mixed + out_bias.astype(jnp.float32)
    return (normed_low, query, keys, values, context_low, lse_blocks, middle, slopes)


def mlp_front(middle, second_gain, second_shift, up_weight, up_bias):
    second_low = layer_norm(
        middle, second_gain.astype(jnp.float32), second_shift.astype(jnp.float32)
    ).astype(jnp.bfloat16)
    upper = jnp.dot(second_low, up_weight, preferred_element_type=jnp.float32) + up_bias.astype(
        jnp.float32
    )
    hidden_low = gelu_tanh(upper).astype(jnp.bfloat16)
    return (second_low, upper, hidden_low)


def norm_pull(values, gain_vec, shift_vec, grad_norm):
    norm_value, pull_fn = jax.vjp(
        layer_norm, values, gain_vec.astype(jnp.float32), shift_vec.astype(jnp.float32)
    )
    return pull_fn(grad_norm)


def per_device(
    tokens,
    segment_ids,
    first_gain,
    first_shift,
    qkv_weight,
    qv_bias,
    out_weight,
    out_bias,
    second_gain,
    second_shift,
    up_weight,
    up_bias,
    down_weight,
    down_bias,
    cotangent,
):
    tokens_f = tokens.astype(jnp.float32)
    seg_row = segment_ids[0]
    saved = attn_front(
        tokens_f, seg_row, first_gain, first_shift, qkv_weight, qv_bias, out_weight, out_bias
    )
    middle = saved[6]
    second_low, upper, hidden_low = mlp_front(middle, second_gain, second_shift, up_weight, up_bias)
    part_down = jnp.dot(hidden_low, down_weight, preferred_element_type=jnp.float32).astype(
        jnp.bfloat16
    )
    feed = lax.psum(part_down, "tensor").astype(jnp.float32)
    output = (middle + feed + down_bias.astype(jnp.float32)).astype(jnp.bfloat16)
    normed_low, query, keys, values, context_low, lse_blocks, middle, slopes = saved
    grad_out = cotangent.astype(jnp.float32)
    grad_down_weight = jnp.einsum(
        "tf,td->fd", hidden_low, cotangent, preferred_element_type=jnp.float32
    )
    grad_down_bias = jnp.sum(grad_out, axis=0)
    grad_hidden = jnp.einsum(
        "td,fd->tf", cotangent, down_weight, preferred_element_type=jnp.float32
    )
    gelu_value, gelu_pull = jax.vjp(gelu_tanh, upper)
    grad_upper_low = gelu_pull(grad_hidden)[0].astype(jnp.bfloat16)
    grad_up_bias = jnp.sum(grad_upper_low.astype(jnp.float32), axis=0)
    grad_up_weight = jnp.einsum(
        "td,tf->df", second_low, grad_upper_low, preferred_element_type=jnp.float32
    )
    part_second = jnp.einsum(
        "tf,df->td", grad_upper_low, up_weight, preferred_element_type=jnp.float32
    )
    grad_second = lax.psum(part_second.astype(jnp.bfloat16), "tensor").astype(jnp.float32)
    grad_middle_norm, grad_second_gain, grad_second_shift = norm_pull(
        middle, second_gain, second_shift, grad_second
    )
    grad_middle = grad_out + grad_middle_norm
    mlp_grads = (
        lax.psum(grad_down_weight.astype(jnp.bfloat16), "dp").astype(jnp.float32),
        lax.psum(grad_up_weight.astype(jnp.bfloat16), "dp").astype(jnp.float32),
        lax.psum(grad_up_bias.astype(jnp.bfloat16), "dp").astype(jnp.float32),
        lax.psum(grad_down_bias.astype(jnp.bfloat16), "dp").astype(jnp.float32),
        lax.psum(grad_second_gain.astype(jnp.bfloat16), "dp").astype(jnp.float32),
        lax.psum(grad_second_shift.astype(jnp.bfloat16), "dp").astype(jnp.float32),
    )
    grad_middle_low = grad_middle.astype(jnp.bfloat16)
    grad_out_bias = jnp.sum(grad_middle, axis=0)
    grad_out_weight = jnp.einsum(
        "tc,td->cd", context_low, grad_middle_low, preferred_element_type=jnp.float32
    )
    grad_context = jnp.einsum(
        "td,cd->tc", grad_middle_low, out_weight, preferred_element_type=jnp.float32
    )
    grad_context = grad_context.astype(jnp.bfloat16).reshape(query.shape)
    grad_query, grad_keys, grad_values = attend_backward(
        query, keys, values, seg_row, slopes, lse_blocks, grad_context
    )
    grad_query_low = grad_query.astype(jnp.bfloat16)
    grad_values_low = grad_values.astype(jnp.bfloat16)
    grad_merged = jnp.concatenate(
        [grad_query_low, grad_keys.astype(jnp.bfloat16), grad_values_low], axis=2
    )
    grad_qv_bias = jnp.concatenate(
        [
            jnp.sum(grad_query_low.astype(jnp.float32), axis=0),
            jnp.sum(grad_values_low.astype(jnp.float32), axis=0),
        ],
        axis=1,
    )
    grad_qkv_weight = jnp.einsum(
        "td,the->dhe", normed_low, grad_merged, preferred_element_type=jnp.float32
    )
    part_first = jnp.einsum(
        "the,dhe->td", grad_merged, qkv_weight, preferred_element_type=jnp.float32
    )
    grad_first = lax.psum(part_first.astype(jnp.bfloat16), "tensor").astype(jnp.float32)
    grad_tokens_norm, grad_first_gain, grad_first_shift = norm_pull(
        tokens_f, first_gain, first_shift, grad_first
    )
    grad_tokens_f = grad_middle + grad_tokens_norm
    grad_tokens = grad_tokens_f.astype(jnp.bfloat16)
    attn_grads = (
        lax.psum(grad_qkv_weight.astype(jnp.bfloat16), "dp").astype(jnp.float32),
        lax.psum(grad_qv_bias.astype(jnp.bfloat16), "dp").astype(jnp.float32),
        lax.psum(grad_out_weight.astype(jnp.bfloat16), "dp").astype(jnp.float32),
        lax.psum(grad_out_bias.astype(jnp.bfloat16), "dp").astype(jnp.float32),
        lax.psum(grad_first_gain.astype(jnp.bfloat16), "dp").astype(jnp.float32),
        lax.psum(grad_first_shift.astype(jnp.bfloat16), "dp").astype(jnp.float32),
    )
    return (
        output,
        grad_tokens,
        attn_grads[4],
        attn_grads[5],
        attn_grads[0],
        attn_grads[1],
        attn_grads[2],
        attn_grads[3],
        mlp_grads[4],
        mlp_grads[5],
        mlp_grads[1],
        mlp_grads[2],
        mlp_grads[0],
        mlp_grads[3],
    )


def solution(mesh):
    return jax.shard_map(
        per_device,
        mesh=mesh,
        in_specs=(
            P("dp", None),
            P("dp", None),
            P(),
            P(),
            P(None, "tensor", None),
            P("tensor", None),
            P("tensor", None),
            P(),
            P(),
            P(),
            P(None, "tensor"),
            P("tensor"),
            P("tensor", None),
            P(),
            P("dp", None),
        ),
        out_specs=(
            P("dp", None),
            P("dp", None),
            P(),
            P(),
            P(None, "tensor", None),
            P("tensor", None),
            P("tensor", None),
            P(),
            P(),
            P(),
            P(None, "tensor"),
            P("tensor"),
            P("tensor", None),
            P(),
        ),
        check_vma=False,
    )
```

profile of v0, /device:TPU:0, one launch (start us, length us, event | category | flops | bytes accessed | tf_op | source)
XLA Modules:
  0.0 955.8 jit_solution(13853205372670522851)
XLA Ops:
  9.8 2.8 convert_reduce_fusion
  21.4 48.7 %while.28 = (s32[]{:T(128)}, bf16[4,512,2,64]{1,3,2,0:T(8,128)(2,1)S(1)}, f32[4,2,512]{2,1,0:T(2,128)S(1)}, s32[4]{0:T(128)S(1)}, s32[2048]{0:T(1024)S(1)}, /*in...) while((s32[]{:T(128)}, ...), condition=%wide.region_5.6_spmd.clone, body=%wide.region_2.5_spmd.clone.sunk | while | flops 579862016 | bytes 47633644 | solution.py:63
  27.1 3.2 fusion.131
  30.3 3.2 fusion.132
  39.3 3.2 fusion.131
  42.5 3.2 fusion.132
  51.4 3.2 fusion.131
  54.6 3.2 fusion.132
  60.8 2.8 fusion.130
  63.5 3.2 fusion.131
  66.7 3.2 fusion.132
  70.7 3.3 convolution_convert_fusion.2
  74.8 158.6 %all-reduce.8.cloned.1.call-done = bf16[2048,1024]{1,0:T(8,128)(2,1)} async-done(((bf16[2048,1024]{1,0:T(8,128)(2,1)}), bf16[2048,1024]{1,0:T(8,128)(2,1)}) %all-reduce.8.cloned.1.call-update) | async-done | bytes 4194320 | tf_op jit(solution)/shard_map/psum | solution.py:125
  233.3 5.0 fusion.54
  241.4 3.5 fusion.73
  244.9 6.4 fusion.76
  252.7 4.4 convolution_convert_fusion
  257.4 7.1 convolution_convert_fusion.4
  265.3 4.5 convolution_convert_fusion.5
  269.8 142.9 %all-reduce.10.cloned.1.call-done = bf16[2048,1024]{1,0:T(8,128)(2,1)} async-done(((bf16[2048,1024]{1,0:T(8,128)(2,1)}), bf16[2048,1024]{1,0:T(8,128)(2,1)}) %all-reduce.10.cloned.1.call-update) | async-done | bytes 4194320 | tf_op jit(solution)/shard_map/psum | solution.py:195
  412.7 6.8 fusion.47
  421.0 6.9 fusion.48
  427.9 5.7 fusion.78
  440.1 117.1 %while.29 = (s32[]{:T(128)}, f32[2048,2,64]{0,2,1:T(8,128)S(1)}, f32[2048,2,64]{0,2,1:T(8,128)}, bf16[4,512,2,64]{1,3,2,0:T(8,128)(2,1)}, s32[4]{0:T(128)S(1)}, ...) while((s32[]{:T(128)}, f32[2048,2,64]{0,2,1:T(8,128)S(1)}, ...), condition=%wide.region_15.16_spmd.clone, body=%wide.region_13.15_spmd.clone.sunk | while | flops 1371864576 | bytes 145007648 | solution.py:100
  447.6 6.2 multiply_reduce_fusion.3
  453.8 8.7 multiply_convert_fusion.5
  462.5 4.6 fusion.145
  476.8 6.2 multiply_reduce_fusion.3
  483.0 8.7 multiply_convert_fusion.5
  491.7 4.6 fusion.145
  505.9 6.2 multiply_reduce_fusion.3
  512.2 8.7 multiply_convert_fusion.5
  520.8 4.6 fusion.145
  535.1 6.2 multiply_reduce_fusion.3
  541.3 8.7 multiply_convert_fusion.5
  550.0 4.6 fusion.145
  563.2 7.1 convolution_convert_fusion.1
  570.3 4.4 bitcast_convert_fusion
  574.7 3.0 reduce_sum.218
  577.7 2.9 reduce_sum.213
  580.9 49.7 %all-reduce.14.cloned.1.call-done = (bf16[1024,2,192]{0,2,1:T(8,128)(2,1)}, bf16[128,1024]{1,0:T(8,128)(2,1)}, bf16[1024,512]{1,0:T(8,128)(2,1)}, bf16[512,1024]{1,0:T(8,128)(2,1)}) async-done(((bf16[1024,2,192]{0,2,1:T(8,128)(2,1)}, bf16[128,1024]{1,0:T(8,128)(2,1)}, bf16[1024,512]{1,0:T(8,128)(2,1)}, bf16[512,1024]{1,0:T(8,128)(2,1)}), (bf16[1024,2,192]{0,2,1:T(8,128)(2,1)}, bf16[128,1024]{1,0:T(8,128)(2,1)}, ...) | async-done | bytes 3145744 | tf_op jit(solution)/shard_map/psum | solution.py:245
  634.9 2.8 convert_element_type.253
  639.3 265.9 %all-reduce.12.cloned.1.call-done = (bf16[2048,1024]{1,0:T(8,128)(2,1)}, bf16[2048,1024]{1,0:T(8,128)(2,1)}) async-done(((bf16[2048,1024]{1,0:T(8,128)(2,1)}, bf16[2048,1024]{1,0:T(8,128)(2,1)}), (bf16[2048,1024]{1,0:T(8,128)(2,1)}, bf16[2048,1024]{1,0:T(8,128)(2,1)})) %all-reduce.12.cloned.1.call-update) | async-done | bytes 8388624 | tf_op jit(solution)/shard_map/psum | solution.py:175
  905.2 4.5 fusion.51
  909.7 2.9 reduce_sum.205
  912.7 6.8 fusion.49
  919.5 10.8 %all-reduce.1 = (bf16[1024]{0:T(1024)(128)(2,1)S(1)}, bf16[1024]{0:T(1024)(128)(2,1)S(1)}, bf16[2,128]{1,0:T(2,128)(2,1)S(1)}, bf16[1024]{0:T(1024)(128)(2,1)S(1...) all-reduce(bf16[1024]{0:T(1024)(128)(2,1)S(1)} %get-tuple-element.2, ...), channel_id=1, replica_groups=mesh['dp'=4,'tensor'=8] {'dp'}, use_global_device_ids=true, to_apply=%region_20.21 | all-reduce | flops 6912 | bytes 27648 | tf_op jit(solution)/shard_map/psum | solution.py:249
  935.0 14.1 %add_convert_fusion = (bf16[2048,1024]{1,0:T(8,128)(2,1)}, bf16[2048,1024]{1,0:T(8,128)(2,1)}) fusion(f32[2048,1024]{1,0:T(8,128)} %copy-done.10, bf16[2048,1024]{1,0:T(8,128)(2,1)} %param.19, bf16[2048,1024]{1,0:T(8,128)(2,1)} %get-tuple-element.260, f32[2048]{0:T(1024)S(1)} %negate_multiply_fusion, f32[2048]{0:T(1024)S(1)} %multiply_multiply_fusion.2, ...), kind=kLoop, calls=%fused_computation.75 | loop fusion | flops 37748736 | bytes 33599488 | tf_op jit(solution)/shard_map/convert_element_type | solution.py:243
  (283 shorter events, 88.0 us)
Async XLA Ops:
  7.2 237.7 %copy-start = (bf16[512,1024]{1,0:T(8,128)(2,1)S(1)}, bf16[512,1024]{1,0:T(8,128)(2,1)}, u32[]{:S(2)}) copy-start(bf16[512,1024]{1,0:T(8,128)(2,1)} %param.31) | copy-start | bytes 3145732
  7.2 226.1 %all-reduce.8.cloned.1.call-start = ((), (), s32[]{:S(2)}) async-start(), calls=%async_computation | async-start | bytes 8388608 | tf_op jit(solution)/shard_map/psum | solution.py:125
  7.3 5.4 copy-start.3
  9.1 5.0 copy-start.35
  21.4 49.3 %copy-start.28 = (bf16[128,1024]{1,0:T(8,128)(2,1)S(1)}, bf16[128,1024]{1,0:T(8,128)(2,1)}, u32[]{:S(2)}) copy-start(bf16[128,1024]{1,0:T(8,128)(2,1)} %param.25) | copy-start | bytes 786436
  70.2 3.9 copy-start.16
  74.1 338.6 %all-reduce.10.cloned.1.call-start = ((), (), s32[]{:S(2)}) async-start(), calls=%async_computation.1 | async-start | bytes 8388608 | tf_op jit(solution)/shard_map/psum | solution.py:195
  74.7 182.7 %copy-start.45 = (f32[512]{0:T(512)}, f32[512]{0:T(512)S(1)}, u32[]{:S(2)}) copy-start(f32[512]{0:T(512)S(1)} %convert_element_type.218) | copy-start | bytes 6148
  74.7 353.2 %copy-start.31 = (f32[1024]{0:T(1024)}, f32[1024]{0:T(1024)S(1)}, u32[]{:S(2)}) copy-start(f32[1024]{0:T(1024)S(1)} %convert_element_type.214) | copy-start | bytes 12292
  233.3 5.0 copy-start.4
  233.3 5.9 copy-start.7
  241.4 3.5 copy-start.14
  244.9 6.4 copy-start.54
  257.1 373.4 %all-reduce.14.cloned.1.call-start = ((), (), s32[]{:S(2)}) async-start(), calls=%async_computation.3 | async-start | bytes 6291456 | tf_op jit(solution)/shard_map/psum | solution.py:245
  257.4 7.1 copy-start.5
  257.4 7.1 copy-start.8
  257.4 7.9 copy-start.53
  412.7 6.8 copy-start.6
  412.7 7.1 copy-start.9
  412.7 8.3 copy-start.11
  421.0 6.9 copy-start.15
  427.9 5.7 copy-start.19
  447.6 6.2 copy-start.1
  453.8 8.7 copy-start.12
  462.5 4.6 copy-start.2
  462.5 4.8 copy-start.20
  476.8 6.2 copy-start.1
  483.0 8.7 copy-start.12
  491.7 4.6 copy-start.2
  491.7 4.8 copy-start.20
  505.9 6.2 copy-start.1
  512.2 8.7 copy-start.12
  520.8 4.6 copy-start.2
  520.8 4.8 copy-start.20
  535.1 6.2 copy-start.1
  541.3 8.7 copy-start.12
  550.0 4.6 copy-start.2
  550.0 4.8 copy-start.20
  562.9 7.4 copy-start.51
  562.9 342.3 %all-reduce.12.cloned.1.call-start = ((), (), s32[]{:S(2)}) async-start(), calls=%async_computation.2 | async-start | bytes 16777216 | tf_op jit(solution)/shard_map/psum | solution.py:175
  574.7 5.9 copy-start.22
  630.6 7.2 copy-start.27
  632.5 272.8 %copy-start.30 = (f32[2048]{0:T(1024)S(1)}, f32[2048]{0:T(1024)}, u32[]{:S(2)}) copy-start(f32[2048]{0:T(1024)} %copy-done.29) | copy-start | bytes 24580
  632.5 272.8 %copy-start.36 = (f32[1024]{0:T(1024)S(1)}, f32[1024]{0:T(1024)}, u32[]{:S(2)}) copy-start(f32[1024]{0:T(1024)} %copy-done.35) | copy-start | bytes 12292
  912.6 6.9 copy-start.39
  912.6 6.9 copy-start.40
  912.6 6.8 copy-start.48
  912.7 22.3 %copy-start.32 = (f32[1024]{0:T(1024)S(1)}, f32[1024]{0:T(1024)}, u32[]{:S(2)}) copy-start(f32[1024]{0:T(1024)} %copy-done.31) | copy-start | bytes 12292
  (32 other events, 64.1 us)
Sparse Core Ops, SparseCore 0:
  74.2 159.0 all-reduce.7
  257.2 155.3 all-reduce.9
  563.0 67.4 all-reduce.13
  635.1 270.0 all-reduce.11
where the time goes:
time: 964 us; the launch traced here: 956 us
  waiting for transfers between devices  617 us (64%)
  other arithmetic  146 us (15%)
  matrix products  134 us (14%)
  local copies, waits for them, and re-layouts  18.3 us (2%)
  between operations  14.6 us (2%)
  loops' own time  14.3 us (1%)
  blocking collectives  10.8 us (1%)
    psum x1, waiting for transfers between devices, per_device(): feed = lax.psum(part_down, 'tensor').astype(jnp.float32)  266 us
    psum x1, waiting for transfers between devices, attn_front(): mixed = lax.psum(partial_out, 'tensor').astype(jnp.float32)  159 us
    psum x1, waiting for transfers between devices, per_device(): lax.psum(part_second.astype(jnp.bfloat16), 'tensor').astype(jnp.float32)  143 us
    psum x1, waiting for transfers between devices, per_device(): lax.psum(grad_qkv_weight.astype(jnp.bfloat16), 'dp').astype(jnp.float32)  49.7 us
    dot_general x8, matrix products, block_scores(): jnp.einsum('qhe,khe->hqk', query_blk, keys, preferred_element_type=jnp.fl...  36 us
    convert_element_type x4, other arithmetic, one_block(): grad_scores = (probs * (grad_probs - inner)).astype(jnp.bfloat16)  34.7 us
    reduce_sum x6, other arithmetic, layer_norm(): return offset * lax.rsqrt(spread + norm_eps) * gain_vec + shift_vec  30.7 us
  transfers between devices with their start and end apart: 4, of which 4 were waited for; matrix products, arithmetic and copies ran while one was open for 4% of the time, Pallas kernels for 0%

commit v1 on v0

--- a/solution.py
+++ b/solution.py
@@ -1,3 +1,4 @@
+import functools
 import math
 import jax
 import jax.numpy as jnp
@@ -5,6 +6,14 @@
 from jax.sharding import PartitionSpec as P
 
 norm_eps = 1e-05
+
+
+def prepare_the_things(here_x, comm_axis):
+    small = lax.all_gather(here_x, comm_axis).sum(axis=0)
+    return small
+
+
+group_the_tasks = functools.partial(prepare_the_things, comm_axis="dp")
 
 
 def layer_norm(values, gain_vec, shift_vec):
@@ -242,7 +251,7 @@
     grad_tokens_f = grad_middle + grad_tokens_norm
     grad_tokens = grad_tokens_f.astype(jnp.bfloat16)
     attn_grads = (
-        lax.psum(grad_qkv_weight.astype(jnp.bfloat16), "dp").astype(jnp.float32),
+        group_the_tasks(grad_qkv_weight.astype(jnp.bfloat16)).astype(jnp.float32),
         lax.psum(grad_qv_bias.astype(jnp.bfloat16), "dp").astype(jnp.float32),
         lax.psum(grad_out_weight.astype(jnp.bfloat16), "dp").astype(jnp.float32),
         lax.psum(grad_out_bias.astype(jnp.bfloat16), "dp").astype(jnp.float32),

time: 964 us -> 930 us (0.965)
  waiting for transfers between devices: 617 us -> 566 us
    psum x1, waiting for transfers between devices: 49.7 us -> 0.01 us  [per_device(): lax.psum(grad_out_weight.astype(jnp.bfloat16), 'dp').astype(jnp.float32)]
  transfers between devices with their start and end apart: 4 -> 5, of which waited for: 4 -> 4; matrix products, arithmetic and copies ran while one was open for 4% -> 17% of each run, Pallas kernels for 0% -> 0%
where the time goes in v1:
time: 930 us; the launch traced here: 921 us
  waiting for transfers between devices  566 us (61%)
  other arithmetic  151 us (16%)
  matrix products  137 us (15%)
  local copies, waits for them, and re-layouts  26.4 us (3%)
  between operations  14.8 us (2%)
  loops' own time  13.9 us (1%)
  blocking collectives  10.8 us (1%)
    psum x1, waiting for transfers between devices, per_device(): feed = lax.psum(part_down, 'tensor').astype(jnp.float32)  261 us
    psum x1, waiting for transfers between devices, attn_front(): mixed = lax.psum(partial_out, 'tensor').astype(jnp.float32)  159 us
    psum x1, waiting for transfers between devices, per_device(): lax.psum(part_second.astype(jnp.bfloat16), 'tensor').astype(jnp.float32)  143 us
    dot_general x8, matrix products, block_scores(): jnp.einsum('qhe,khe->hqk', query_blk, keys, preferred_element_type=jnp.fl...  36 us
    convert_element_type x4, other arithmetic, one_block(): grad_scores = (probs * (grad_probs - inner)).astype(jnp.bfloat16)  35 us
    reduce_sum x6, other arithmetic, layer_norm(): return offset * lax.rsqrt(spread + norm_eps) * gain_vec + shift_vec  30.8 us
  transfers between devices with their start and end apart: 5, of which 4 were waited for; matrix products, arithmetic and copies ran while one was open for 17% of the time, Pallas kernels for 0%

profile of v1, /device:TPU:0, one launch (start us, length us, event | category | flops | bytes accessed | tf_op | source)
XLA Modules:
  0.0 921.1 jit_solution(17429748635721791085)
XLA Ops:
  21.4 48.8 %while.28 = (s32[]{:T(128)}, bf16[4,512,2,64]{1,3,2,0:T(8,128)(2,1)S(1)}, f32[4,2,512]{2,1,0:T(2,128)S(1)}, s32[4]{0:T(128)S(1)}, s32[2048]{0:T(1024)S(1)}, /*in...) while((s32[]{:T(128)}, ...), condition=%wide.region_5.6_spmd.clone, body=%wide.region_2.5_spmd.clone.sunk | while | flops 579862016 | bytes 47633644 | solution.py:72
  27.1 3.2 fusion.131
  30.3 3.2 fusion.132
  39.3 3.2 fusion.131
  42.5 3.2 fusion.132
  51.4 3.2 fusion.131
  54.6 3.2 fusion.132
  63.5 3.2 fusion.131
  66.8 3.2 fusion.132
  70.8 3.3 convolution_convert_fusion.2
  74.8 158.6 %all-reduce.8.cloned.1.call-done = bf16[2048,1024]{1,0:T(8,128)(2,1)} async-done(((bf16[2048,1024]{1,0:T(8,128)(2,1)}), bf16[2048,1024]{1,0:T(8,128)(2,1)}) %all-reduce.8.cloned.1.call-update) | async-done | bytes 4194320 | tf_op jit(solution)/shard_map/psum | solution.py:134
  233.4 5.0 fusion.54
  241.5 3.5 fusion.73
  245.0 6.4 fusion.76
  252.7 4.4 convolution_convert_fusion
  257.8 7.1 convolution_convert_fusion.4
  265.6 4.5 convolution_convert_fusion.5
  270.1 142.6 %all-reduce.10.cloned.1.call-done = bf16[2048,1024]{1,0:T(8,128)(2,1)} async-done(((bf16[2048,1024]{1,0:T(8,128)(2,1)}), bf16[2048,1024]{1,0:T(8,128)(2,1)}) %all-reduce.10.cloned.1.call-update) | async-done | bytes 4194320 | tf_op jit(solution)/shard_map/psum | solution.py:204
  412.7 6.8 fusion.47
  421.0 6.9 fusion.48
  428.0 5.7 fusion.78
  433.6 3.2 copy-done.10
  438.3 5.7 convolution_convert_fusion.3
  445.1 117.2 %while.29 = (s32[]{:T(128)}, f32[2048,2,64]{0,2,1:T(8,128)S(1)}, f32[2048,2,64]{0,2,1:T(8,128)}, bf16[4,512,2,64]{1,3,2,0:T(8,128)(2,1)}, s32[4]{0:T(128)S(1)}, ...) while((s32[]{:T(128)}, f32[2048,2,64]{0,2,1:T(8,128)S(1)}, ...), condition=%wide.region_15.16_spmd.clone, body=%wide.region_13.15_spmd.clone.sunk | while | flops 1371864576 | bytes 145007648 | solution.py:109
  452.2 6.2 multiply_reduce_fusion.3
  458.4 8.8 multiply_convert_fusion.5
  467.2 4.7 fusion.145
  481.7 6.2 multiply_reduce_fusion.3
  487.9 8.8 multiply_convert_fusion.5
  496.7 4.6 fusion.145
  511.0 6.2 multiply_reduce_fusion.3
  517.2 8.7 multiply_convert_fusion.5
  525.9 4.6 fusion.145
  540.2 6.2 multiply_reduce_fusion.3
  546.4 8.7 multiply_convert_fusion.5
  555.1 4.6 fusion.145
  568.1 7.2 convolution_convert_fusion.1
  575.2 4.4 bitcast_convert_fusion
  579.7 3.0 reduce_sum.260
  592.1 3.6 all-gather.3.cloned.1.call-done
  595.7 6.3 reshape.277
  602.0 5.7 reduce_sum.220
  609.0 261.2 %all-reduce.12.cloned.1.call-done = (bf16[2048,1024]{1,0:T(8,128)(2,1)}, bf16[2048,1024]{1,0:T(8,128)(2,1)}) async-done(((bf16[2048,1024]{1,0:T(8,128)(2,1)}, bf16[2048,1024]{1,0:T(8,128)(2,1)}), (bf16[2048,1024]{1,0:T(8,128)(2,1)}, bf16[2048,1024]{1,0:T(8,128)(2,1)})) %all-reduce.12.cloned.1.call-update) | async-done | bytes 8388624 | tf_op jit(solution)/shard_map/psum | solution.py:184
  870.2 4.5 fusion.51
  874.7 2.9 reduce_sum.219
  877.7 6.8 fusion.49
  884.5 10.8 %all-reduce.1 = (bf16[1024]{0:T(1024)(128)(2,1)S(1)}, bf16[1024]{0:T(1024)(128)(2,1)S(1)}, bf16[2,128]{1,0:T(2,128)(2,1)S(1)}, bf16[1024]{0:T(1024)(128)(2,1)S(1...) all-reduce(bf16[1024]{0:T(1024)(128)(2,1)S(1)} %get-tuple-element.2, ...), channel_id=1, replica_groups=mesh['dp'=4,'tensor'=8] {'dp'}, use_global_device_ids=true, to_apply=%region_20.21 | all-reduce | flops 6912 | bytes 27648 | tf_op jit(solution)/shard_map/psum | solution.py:258
  900.0 14.1 %add_convert_fusion = (bf16[2048,1024]{1,0:T(8,128)(2,1)}, bf16[2048,1024]{1,0:T(8,128)(2,1)}) fusion(f32[2048,1024]{1,0:T(8,128)} %copy-done.10, bf16[2048,1024]{1,0:T(8,128)(2,1)} %param.19, bf16[2048,1024]{1,0:T(8,128)(2,1)} %get-tuple-element.260, f32[2048]{0:T(1024)S(1)} %negate_multiply_fusion, f32[2048]{0:T(1024)S(1)} %multiply_multiply_fusion.2, ...), kind=kLoop, calls=%fused_computation.75 | loop fusion | flops 37748736 | bytes 33599488 | tf_op jit(solution)/shard_map/convert_element_type | solution.py:252
  (288 shorter events, 94.2 us)
Async XLA Ops:
  7.2 237.8 %copy-start = (bf16[512,1024]{1,0:T(8,128)(2,1)S(1)}, bf16[512,1024]{1,0:T(8,128)(2,1)}, u32[]{:S(2)}) copy-start(bf16[512,1024]{1,0:T(8,128)(2,1)} %param.31) | copy-start | bytes 3145732
  7.2 226.2 %all-reduce.8.cloned.1.call-start = ((), (), s32[]{:S(2)}) async-start(), calls=%async_computation | async-start | bytes 8388608 | tf_op jit(solution)/shard_map/psum | solution.py:134
  7.3 5.4 copy-start.3
  9.1 5.0 copy-start.35
  21.4 49.3 %copy-start.28 = (bf16[128,1024]{1,0:T(8,128)(2,1)S(1)}, bf16[128,1024]{1,0:T(8,128)(2,1)}, u32[]{:S(2)}) copy-start(bf16[128,1024]{1,0:T(8,128)(2,1)} %param.25) | copy-start | bytes 786436
  70.2 3.9 copy-start.16
  74.1 338.6 %all-reduce.10.cloned.1.call-start = ((), (), s32[]{:S(2)}) async-start(), calls=%async_computation.1 | async-start | bytes 8388608 | tf_op jit(solution)/shard_map/psum | solution.py:204
  74.8 183.0 %copy-start.45 = (f32[512]{0:T(512)}, f32[512]{0:T(512)S(1)}, u32[]{:S(2)}) copy-start(f32[512]{0:T(512)S(1)} %convert_element_type.220) | copy-start | bytes 6148
  74.8 353.2 %copy-start.31 = (f32[1024]{0:T(1024)}, f32[1024]{0:T(1024)S(1)}, u32[]{:S(2)}) copy-start(f32[1024]{0:T(1024)S(1)} %convert_element_type.216) | copy-start | bytes 12292
  233.4 5.0 copy-start.4
  233.4 5.9 copy-start.7
  245.0 6.4 copy-start.54
  257.2 328.6 %all-reduce.14.cloned.1.call-start = ((), (), s32[]{:S(2)}) async-start(), calls=%async_computation.4 | async-start | bytes 4718592 | tf_op jit(solution)/shard_map/psum | solution.py:256
  257.7 7.1 copy-start.5
  257.8 7.1 copy-start.8
  257.8 7.9 copy-start.53
  412.7 6.9 copy-start.6
  412.7 7.1 copy-start.9
  412.7 8.3 copy-start.11
  421.0 6.9 copy-start.15
  427.9 8.9 copy-start.19
  444.0 151.7 %all-gather.3.cloned.1.call-start = ((), (), s32[]{:S(2)}) async-start(), calls=%async_computation.2 | async-start | bytes 3932160 | tf_op jit(solution)/shard_map/all_gather | solution.py:12
  452.2 6.2 copy-start.1
  458.4 8.8 copy-start.12
  467.2 4.8 copy-start.2
  467.2 4.9 copy-start.20
  481.7 6.2 copy-start.1
  487.9 8.8 copy-start.12
  496.7 4.6 copy-start.2
  496.7 4.8 copy-start.20
  511.0 6.2 copy-start.1
  517.2 8.7 copy-start.12
  525.9 4.6 copy-start.2
  525.9 4.8 copy-start.20
  540.2 6.2 copy-start.1
  546.4 8.7 copy-start.12
  555.1 4.6 copy-start.2
  555.1 4.8 copy-start.20
  568.0 7.2 copy-start.51
  568.0 302.2 %all-reduce.12.cloned.1.call-start = ((), (), s32[]{:S(2)}) async-start(), calls=%async_computation.3 | async-start | bytes 16777216 | tf_op jit(solution)/shard_map/psum | solution.py:184
  579.7 5.9 copy-start.22
  585.8 4.7 copy-start.27
  602.0 268.2 %copy-start.30 = (f32[2048]{0:T(1024)S(1)}, f32[2048]{0:T(1024)}, u32[]{:S(2)}) copy-start(f32[2048]{0:T(1024)} %copy-done.29) | copy-start | bytes 24580
  602.0 268.2 %copy-start.36 = (f32[1024]{0:T(1024)S(1)}, f32[1024]{0:T(1024)}, u32[]{:S(2)}) copy-start(f32[1024]{0:T(1024)} %copy-done.35) | copy-start | bytes 12292
  877.6 6.9 copy-start.39
  877.6 6.9 copy-start.40
  877.7 6.8 copy-start.48
  877.7 22.3 %copy-start.32 = (f32[1024]{0:T(1024)S(1)}, f32[1024]{0:T(1024)}, u32[]{:S(2)}) copy-start(f32[1024]{0:T(1024)} %copy-done.31) | copy-start | bytes 12292
  (33 other events, 69.2 us)
Sparse Core Ops, SparseCore 0:
  74.3 159.0 all-reduce.7
  257.3 155.3 all-reduce.9
  444.1 54.6 all-reduce.13
  568.1 27.5 all-gather.2
  600.2 270.0 all-reduce.11
